TPU v7x, 32 devices: a whole 2x2x4 slice. The times are simulated.
32 devices in a mesh: pole: 2 (over x), row: 8 (over z, y), col: 2 (over core).
Axes of the slice: x: 2, y: 2, z: 4, core: 2. Of those that a mesh axis runs over, the one named last changes fastest.
Arguments:
- inverse_pairs: bfloat16 [4, 12288, 12288], P('pole', 'row', 'col'), parts along dimension 0, may hold values from -0.09375 to 0.09375
- factor_rows: bfloat16 [4, 2, 2048, 256], P('pole', None, 'row', 'col'), parts along dimension 0, may hold values from -1.1953125 to 1.1953125
- diag_blocks: bfloat16 [4, 2, 256, 256], P('pole', None, None, 'col'), parts along dimension 0, may hold values from -6 to 6
- row_lists: int32 [2, 16], replicated, may hold values from 0 to 95, as said below
- block_order: int32 [96], replicated, may hold values from 0 to 95, each once
Outputs:
- inv_cols: float32 [4, 2, 12288, 256], P('pole', None, 'row', 'col'), parts along dimension 0
- schur_blocks: float32 [4, 2, 256, 256], P('pole', None, None, 'col'), parts along dimension 0
There are 2 independent parts, one for each index of `pole`. A program takes and returns all parts, laid end to end along the dimension named above; an argument that names none is the same for every part. Nothing has to cross between parts.
Inputs may be any that keep to these rules, and one draw needn't show every extreme that they name: `row_lists`: each of the 2 rows holds 16 different block numbers in increasing order, always including 0 and 95.
All inputs are finite; a program needn't handle non-finite values.
Results may differ from a plain program's by a relative error of at most 0.0003.
Values may be sent and summed in bfloat16 or wider, within the bound.
A program may use at most 128 MiB of HBM per device.

v0:
```python
import jax
import jax.numpy as jnp
from jax import lax
from jax.sharding import PartitionSpec as P

NSN = 2
BLK = 128
R = 16
NB = 96


def place_rows(factor_full, row_lists, block_order, first_block, block_count):
    storage = first_block + jnp.arange(block_count, dtype=jnp.int32)
    picked = (jnp.arange(NB, dtype=jnp.int32)[None, :] == storage[:, None]).astype(jnp.int32)
    ancestor = jnp.sum(picked * block_order[None, :], axis=1)
    matches = (row_lists[:, None, :] == ancestor[None, :, None]).astype(jnp.bfloat16)
    blocked = factor_full.reshape(NSN, 2, R, BLK, factor_full.shape[3])
    placed = jnp.einsum("ktj,kpjbw->kptbw", matches, blocked, preferred_element_type=jnp.float32)
    return placed.reshape(NSN, 2, block_count * BLK, factor_full.shape[3])


def complex_gram(row_factor, values):
    terms = jnp.einsum("kpmv,kqmw->kpqvw", row_factor, values, precision=lax.Precision.HIGHEST)
    gram_real = terms[:, 0, 0] - terms[:, 1, 1]
    gram_imag = terms[:, 0, 1] + terms[:, 1, 0]
    return jnp.stack([gram_real, gram_imag], axis=1)


def local(inverse_pairs, factor_rows, diag_blocks, row_lists, block_order):
    local_rows = inverse_pairs.shape[1]
    local_cols = inverse_pairs.shape[2]
    lengthened = lax.all_gather(factor_rows, "row", axis=2, tiled=True)
    factor_full = lax.all_gather(lengthened, "col", axis=3, tiled=True)
    col_block = lax.axis_index("col") * (local_cols // BLK)
    row_block = lax.axis_index("row") * (local_rows // BLK)
    column_factor = place_rows(
        factor_full, row_lists, block_order, col_block, local_cols // BLK
    ).astype(jnp.bfloat16)
    products = jnp.einsum(
        "prc,kqcw->kpqrw", inverse_pairs, column_factor, preferred_element_type=jnp.float32
    )
    partial_real = products[:, 1, 1] - products[:, 0, 0]
    partial_imag = -(products[:, 0, 1] + products[:, 1, 0])
    partial_value = jnp.stack([partial_real, partial_imag], axis=1)
    row_factor = place_rows(factor_full, row_lists, block_order, row_block, local_rows // BLK)
    values = lax.psum_scatter(partial_value, "col", scatter_dimension=3, tiled=True)
    correction = lax.psum(complex_gram(row_factor, values), "row")
    schur = diag_blocks.astype(jnp.float32) - correction
    return (values, schur)


def solution(mesh):
    in_specs = (
        P("pole", "row", "col"),
        P("pole", None, "row", "col"),
        P("pole", None, None, "col"),
        P(),
        P(),
    )
    out_specs = (P("pole", None, "row", "col"), P("pole", None, None, "col"))
    return jax.shard_map(local, mesh=mesh, in_specs=in_specs, out_specs=out_specs, check_vma=False)
```

profile of v0, /device:TPU:26, one launch (start us, length us, event | category | flops | bytes accessed | tf_op | source)
XLA Modules:
  0.0 261.6 jit_solution(5159684242705975721)
XLA Ops:
  7.2 0.0 all-gather.3.cloned.1.call-start
  7.2 0.7 all-gather.3.cloned.1.call-update
  7.9 0.0 all-gather.5.cloned.1.call-start
  7.9 50.8 %all-gather.3.cloned.1.call-done = bf16[2,2,2048,128]{3,2,1,0:T(8,128)(2,1)} async-done(((bf16[2,2,256,128]{3,2,1,0:T(8,128)(2,1)}), bf16[2,2,2048,128]{3,2,1,0:T(8,128)(2,1)}) %all-gather.3.cloned.1.call-update) | async-done | bytes 2097168 | tf_op jit(solution)/shard_map/all_gather | solution.py:32
  58.7 0.0 all-gather.5.cloned.1.call-update
  58.8 0.0 reduce-scatter.2.cloned.1.call-start
  58.8 0.8 select_reduce_fusion
  59.7 13.7 %all-gather.5.cloned.1.call-done = bf16[2,2,2048,256]{3,2,1,0:T(8,128)(2,1)} async-done(((bf16[2,2,2048,128]{3,2,1,0:T(8,128)(2,1)}), bf16[2,2,2048,256]{3,2,1,0:T(8,128)(2,1)}) %all-gather.5.cloned.1.call-update) | async-done | bytes 4194320 | tf_op jit(solution)/shard_map/all_gather | solution.py:33
  73.4 10.2 %convert_bitcast_fusion = bf16[2,2,48,128,256]{4,2,3,1,0:T(8,128)(2,1)} fusion(bf16[2,2,16,128,256]{4,3,2,1,0:T(8,128)(2,1)} %bitcast.71, s32[48]{0:T(128)S(1)} %select_reduce_fusion, s32[2,16]{1,0:T(2,128)} %param.8), kind=kOutput, calls=%fused_computation.2 | convolution fusion | flops 207619584 | bytes 16777536 | tf_op jit(solution)/shard_map/ktj,kpjbw->kptbw/dot_general | solution.py:18
  83.6 12.5 %copy.29 = bf16[2,2,48,128,256]{4,3,2,1,0:T(8,128)(2,1)} copy(bf16[2,2,48,128,256]{4,2,3,1,0:T(8,128)(2,1)} %convert_bitcast_fusion) | data formatting | bytes 25165824 | tf_op jit(solution)/shard_map/convert_element_type | solution.py:38
  96.1 48.0 %fusion.2 = f32[2,2,2,1536,256]{3,4,1,2,0:T(8,128)} fusion(bf16[2,2,6144,256,1]{3,2,4,1,0:T(8,128)(2,1)} %bitcast.73, bf16[2,1536,6144]{2,1,0:T(8,128)(2,1)} %param.5), kind=kOutput, calls=%fused_computation.3 | convolution fusion | flops 38654705664 | bytes 62914560 | tf_op jit(solution)/shard_map/prc,kqcw->kpqrw/dot_general | solution.py:39
  144.1 3.5 %fusion.12 = f32[2,1,1536,256]{2,3,0,1:T(8,128)S(1)} fusion(f32[2,2,2,1536,256]{3,4,1,2,0:T(8,128)} %fusion.2), kind=kLoop, calls=%fused_computation.11 | loop fusion | flops 1572864 | bytes 9437184 | tf_op jit(solution)/shard_map/neg | solution.py:43
  147.6 3.4 %fusion.14 = f32[2,1,1536,256]{2,3,0,1:T(8,128)S(1)} fusion(f32[2,2,2,1536,256]{3,4,1,2,0:T(8,128)} %fusion.2), kind=kLoop, calls=%fused_computation.14 | loop fusion | flops 786432 | bytes 9437184 | tf_op jit(solution)/shard_map/sub | solution.py:42
  151.0 3.1 %pad_maximum_fusion = f32[2,2,1536,256]{2,3,0,1:T(8,128)} fusion(f32[2,1,1536,256]{2,3,0,1:T(8,128)S(1)} %fusion.12, f32[2,1,1536,256]{2,3,0,1:T(8,128)S(1)} %fusion.14), kind=kLoop, calls=%fused_computation.4 | loop fusion | flops 1572864 | bytes 12582912 | tf_op jit(solution)/shard_map/stack | solution.py:44
  154.1 0.0 reduce-scatter.2.cloned.1.call-update
  154.1 0.3 all-reduce.2.cloned.1.call-start
  154.4 0.3 copy-done.2
  154.8 0.2 select_reduce_fusion.1
  155.0 0.0 copy-done.1
  155.0 4.8 %fusion.8 = f32[2,2,12,128,256]{4,2,3,1,0:T(8,128)S(1)} fusion(bf16[2,2,16,128,256]{4,3,2,1,0:T(8,128)(2,1)} %bitcast.72, s32[2,16]{1,0:T(2,128)S(1)} %copy-done.1, s32[12]{0:T(128)S(1)} %select_reduce_fusion.1), kind=kOutput, calls=%fused_computation.8 | convolution fusion | flops 50332032 | bytes 10485936 | tf_op jit(solution)/shard_map/ktj,kpjbw->kptbw/dot_general | solution.py:18
  159.7 7.3 %copy.35 = f32[2,2,12,128,256]{4,3,2,1,0:T(8,128)} copy(f32[2,2,12,128,256]{4,2,3,1,0:T(8,128)S(1)} %fusion.8) | data formatting | bytes 12582912 | tf_op jit(solution)/shard_map/ktj,kpjbw->kptbw/transpose | solution.py:18
  167.0 3.4 %reduce-scatter.2.cloned.1.call-done = f32[2,2,1536,128]{2,3,0,1:T(8,128)} async-done(((f32[2,2,1536,256]{2,3,0,1:T(8,128)}), f32[2,2,1536,128]{2,3,0,1:T(8,128)}) %reduce-scatter.2.cloned.1.call-update) | async-done | bytes 3145744 | tf_op jit(solution)/shard_map/reduce_scatter | solution.py:46
  170.4 8.9 %fusion.17 = f32[2,2,2,256,128]{3,4,1,2,0:T(8,128)S(1)} fusion(f32[2,2,1536,256,1]{3,2,1,4,0:T(8,128)} %bitcast.70, f32[2,2,1536,128]{2,3,0,1:T(8,128)} %reduce-scatter.2.cloned.1.call-done), kind=kOutput, calls=%fused_computation.18 | convolution fusion | flops 4831838208 | bytes 10485760 | tf_op jit(solution)/shard_map/kpmv,kqmw->kpqvw/dot_general | solution.py:23
  179.3 0.0 copy-start
  179.4 0.8 pad_maximum_fusion.1
  180.2 0.0 all-reduce.2.cloned.1.call-update
  180.3 1.3 copy.33
  181.5 0.0 copy-done
  181.6 2.4 copy.39
  183.9 69.0 %all-reduce.2.cloned.1.call-done = f32[2,2,256,128]{2,3,0,1:T(8,128)} async-done(((f32[2,2,256,128]{2,3,0,1:T(8,128)}), f32[2,2,256,128]{2,3,0,1:T(8,128)}) %all-reduce.2.cloned.1.call-update) | async-done | bytes 524304 | tf_op jit(solution)/shard_map/psum | solution.py:47
  252.9 1.1 convert_subtract_fusion
  254.0 1.0 copy.40
  (6 shorter events, 0.1 us)
Async XLA Ops:
  7.2 51.6 %all-gather.3.cloned.1.call-start = ((), (), s32[]{:S(2)}) async-start(), calls=%async_computation.1 | async-start | bytes 2359296 | tf_op jit(solution)/shard_map/all_gather | solution.py:32
  7.9 65.5 %all-gather.5.cloned.1.call-start = ((), (), s32[]{:S(2)}) async-start(), calls=%async_computation.2 | async-start | bytes 6291456 | tf_op jit(solution)/shard_map/all_gather | solution.py:33
  58.8 111.6 %reduce-scatter.2.cloned.1.call-start = ((), (), s32[]{:S(2)}) async-start(), calls=%async_computation.3 | async-start | bytes 9437184 | tf_op jit(solution)/shard_map/reduce_scatter | solution.py:46
  154.1 0.7 copy-start.2
  154.1 0.8 copy-start.1
  154.1 98.8 %all-reduce.2.cloned.1.call-start = ((), (), s32[]{:S(2)}) async-start(), calls=%async_computation.4 | async-start | bytes 1048576 | tf_op jit(solution)/shard_map/psum | solution.py:47
  179.3 2.2 copy-start
Sparse Core Ops, SparseCore 0:
  10.2 48.5 all-gather.2
  60.3 13.0 all-gather.4
  154.3 16.0 reduce-scatter.1
  180.4 72.4 all-reduce.1
where the time goes:
time: 265 us; the launch traced here: 262 us
  waiting for transfers between devices  138 us (52%)
  matrix products  72 us (27%)
  local copies, waits for them, and re-layouts  24.8 us (9%)
  between operations  13.9 us (5%)
  other arithmetic  13 us (5%)
    psum x1, waiting for transfers between devices, local(): correction = lax.psum(complex_gram(row_factor, values), 'row')  69 us
    all_gather x1, waiting for transfers between devices, local(): lengthened = lax.all_gather(factor_rows, 'row', axis=2, tiled=True)  50.8 us
    dot_general x1, matrix products, local(): jnp.einsum('prc,kqcw->kpqrw', inverse_pairs, column_factor, preferred_ele...  48 us
    dot_general x2, matrix products, place_rows(): jnp.einsum('ktj,kpjbw->kptbw', matches, blocked, preferred_element_type=j...  15 us
    all_gather x1, waiting for transfers between devices, local(): factor_full = lax.all_gather(lengthened, 'col', axis=3, tiled=True)  13.7 us
    convert_element_type x1, local copies, waits for them, and re-layouts, local(): column_factor = place_rows(factor_full, row_lists, block_order, col_block...  12.5 us
    dot_general x1, matrix products, complex_gram(): jnp.einsum('kpmv,kqmw->kpqvw', row_factor, values, precision=lax.Precisio...  8.94 us
    transpose x1, local copies, waits for them, and re-layouts, place_rows(): jnp.einsum('ktj,kpjbw->kptbw', matches, blocked, preferred_element_type=j...  7.29 us
  transfers between devices with their start and end apart: 4, of which 4 were waited for; matrix products, arithmetic and copies ran while one was open for 6% of the time, Pallas kernels for 0%

commit v1 on v0

v1 whole, which is shorter than its diff:
```python
import functools

import jax
import jax.numpy as jnp
from jax import lax
from jax.experimental import pallas as pl
from jax.experimental.pallas import tpu as pltpu
from jax.sharding import PartitionSpec as P

NSN = 2
BLK = 128
MESH = pl.DeviceIdType.MESH
ANY = pl.BlockSpec(memory_space=pl.ANY)
VMEM = pl.BlockSpec(memory_space=pltpu.VMEM)
SMEM = pl.BlockSpec(memory_space=pltpu.SMEM)


def gather_kernel(n, ny, x_ref, g_ref, loc_sem, zs_send, zs_recv, y_send, y_recv, s_send, s_recv):
    nz = n // ny
    span = x_ref.shape[2]
    row = lax.axis_index("row")
    col = lax.axis_index("col")
    z = row // ny
    y = row % ny
    oy = ny - 1 - y
    sibling = {"col": 1 - col}
    up = {"row": row + ny}
    down = {"row": row - ny}
    across = {"row": z * ny + oy}

    barrier = pltpu.get_barrier_semaphore()
    pl.semaphore_signal(barrier, inc=1, device_id=sibling, device_id_type=MESH)
    pl.semaphore_signal(barrier, inc=1, device_id=across, device_id_type=MESH)

    @pl.when(z < nz - 1)
    def _():
        pl.semaphore_signal(barrier, inc=1, device_id=up, device_id_type=MESH)

    @pl.when(z > 0)
    def _():
        pl.semaphore_signal(barrier, inc=1, device_id=down, device_id_type=MESH)

    pl.semaphore_wait(barrier, 2 + (z < nz - 1).astype(jnp.int32) + (z > 0).astype(jnp.int32))

    def slot(c, r):
        return g_ref.at[c, :, :, pl.ds(pl.multiple_of(r * span, span), span), :]

    def copy(src, c, r, send, recv, target):
        return pltpu.make_async_remote_copy(
            src_ref=src, dst_ref=slot(c, r), send_sem=send, recv_sem=recv,
            device_id=target, device_id_type=MESH,
        )

    def line(src, zz, target):
        return copy(src, col, zz * ny + y, zs_send.at[zz], zs_recv.at[zz], target)

    def side(src, zz, yy):
        return copy(src, col, zz * ny + yy, y_send.at[zz], y_recv.at[zz], across)

    def sib(src, c, r):
        return copy(src, c, r, s_send.at[r], s_recv.at[r], sibling)

    def here(zz, yy):
        return slot(col, zz * ny + yy)

    @pl.when(z < nz - 1)
    def _():
        copy(x_ref, col, row, zs_send.at[nz], zs_recv.at[z], up).start()

    @pl.when(z > 0)
    def _():
        copy(x_ref, col, row, zs_send.at[nz + 1], zs_recv.at[z], down).start()

    side(x_ref, z, y).start()
    sib(x_ref, col, row).start()
    local = pltpu.make_async_copy(x_ref, slot(col, row), loc_sem)
    local.start()

    def from_line(zz, forward, target):
        line(here(zz, y), zz, target).wait_recv()

        @pl.when(forward)
        def _():
            line(here(zz, y), zz, target).start()

        side(here(zz, y), zz, y).start()
        sib(here(zz, y), col, zz * ny + y).start()

    def from_side(zz):
        side(here(zz, oy), zz, oy).wait_recv()
        sib(here(zz, oy), col, zz * ny + oy).start()

    for d in range(1, nz + 1):
        for zz, seen in ((z - d + 1, True), (z + d - 1, d > 1)):
            if seen:
                @pl.when((zz >= 0) & (zz < nz))
                def _():
                    from_side(zz)
        if d < nz:
            @pl.when(z - d >= 0)
            def _():
                from_line(z - d, z < nz - 1, up)

            @pl.when(z + d < nz)
            def _():
                from_line(z + d, z > 0, down)

    local.wait()
    for r in range(n):
        sib(slot(1 - col, r), 1 - col, r).wait_recv()
    for r in range(n):
        sib(slot(col, r), col, r).wait_send()
    for zz in range(nz):
        side(here(zz, y), zz, y).wait_send()

        @pl.when(((zz < z) & (z < nz - 1)) | ((zz > z) & (z > 0)))
        def _():
            line(here(zz, y), zz, up).wait_send()

    @pl.when(z < nz - 1)
    def _():
        copy(x_ref, col, row, zs_send.at[nz], zs_recv.at[z], up).wait_send()

    @pl.when(z > 0)
    def _():
        copy(x_ref, col, row, zs_send.at[nz + 1], zs_recv.at[z], down).wait_send()


def gather(n, x):
    ny = 2 if n % 2 == 0 else 1
    nz = n // ny
    dma = pltpu.SemaphoreType.DMA
    return pl.pallas_call(
        functools.partial(gather_kernel, n, ny),
        out_shape=jax.ShapeDtypeStruct((2, NSN, 2, n * x.shape[2], x.shape[3]), x.dtype),
        in_specs=[ANY],
        out_specs=ANY,
        scratch_shapes=[dma, dma((nz + 2,)), dma((nz,)), dma((nz,)), dma((nz,)), dma((n,)), dma((n,))],
        compiler_params=pltpu.CompilerParams(collective_id=0, has_side_effects=True),
        name="gather_factor",
    )(x)


def product_kernel(listed, blocks_col, blocks_row, meta, g_ref, a_ref, own_ref, oth_ref, gram_ref,
                   abuf, bbuf, entry, sems):
    rows = a_ref.shape[1]
    tile = 256 if rows % 256 == 0 else BLK
    col = meta[2 * NSN, 0]

    def fetch(k, s, block):
        pair = s // 2
        for part in range(2):
            lane = pl.multiple_of((s % 2) * 2 * BLK + part * BLK, BLK)
            pltpu.make_async_copy(
                a_ref.at[part, :, pl.ds(pl.multiple_of(block * BLK, BLK), BLK)],
                abuf.at[k, pair, :, pl.ds(lane, BLK)],
                sems.at[k, pair],
            ).start()

    counts = []
    for k in range(NSN):
        def scan(j, count, k=k):
            block = meta[k, j]
            inside = (block >= 0) & (block < blocks_col)

            @pl.when(inside)
            def _():
                entry[k, count] = j
                fetch(k, count, block)

            return count + inside.astype(jnp.int32)

        count = lax.fori_loop(0, listed, scan, jnp.int32(0))

        @pl.when(count % 2 == 1)
        def _(k=k, count=count):
            fetch(k, count, meta[k, entry[k, count - 1]])

        counts.append(count)

    own_ref[...] = jnp.zeros_like(own_ref)
    oth_ref[...] = jnp.zeros_like(oth_ref)
    gram_ref[...] = jnp.zeros_like(gram_ref)
    outs = (own_ref, oth_ref)
    for k in range(NSN):
        count = counts[k]

        def step(pair, carry, k=k, count=count):
            for half in range(2):
                s = pair * 2 + half
                base = half * 2 * BLK

                @pl.when(s < count)
                def _():
                    at = pl.ds(pl.multiple_of(entry[k, s] * BLK, BLK), BLK)
                    for rel in range(2):
                        c = col if rel == 0 else 1 - col
                        real = g_ref[c, k, 0, at, :]
                        imag = g_ref[c, k, 1, at, :]
                        left = rel * 2 * BLK
                        bbuf[base:base + BLK, left:left + BLK] = -real
                        bbuf[base:base + BLK, left + BLK:left + 2 * BLK] = -imag
                        bbuf[base + BLK:base + 2 * BLK, left:left + BLK] = imag
                        bbuf[base + BLK:base + 2 * BLK, left + BLK:left + 2 * BLK] = -real

                @pl.when(s >= count)
                def _():
                    bbuf[base:base + 2 * BLK, :] = jnp.zeros((2 * BLK, 4 * BLK), jnp.bfloat16)

            pltpu.make_async_copy(abuf.at[k, pair], abuf.at[k, pair], sems.at[k, pair]).wait()

            def by_tile(t, inner):
                at = pl.ds(pl.multiple_of(t * tile, tile), tile)
                left = abuf[k, pair, at, :]
                for rel in range(2):
                    found = jnp.dot(left, bbuf[:, rel * 2 * BLK:(rel + 1) * 2 * BLK],
                                    preferred_element_type=jnp.float32)
                    outs[rel][k, 0, at, :] += found[:, :BLK]
                    outs[rel][k, 1, at, :] += found[:, BLK:]
                return inner

            lax.fori_loop(0, rows // tile, by_tile, 0)
            return carry

        lax.fori_loop(0, (count + 1) // 2, step, 0)

        def correct(j, carry, k=k):
            block = meta[NSN + k, j]

            @pl.when((block >= 0) & (block < blocks_row))
            def _():
                at = pl.ds(pl.multiple_of(j * BLK, BLK), BLK)
                here = pl.ds(pl.multiple_of(block * BLK, BLK), BLK)
                factor = jnp.concatenate([
                    jnp.concatenate([g_ref[0, k, 0, at, :], g_ref[1, k, 0, at, :]], axis=1),
                    jnp.concatenate([g_ref[0, k, 1, at, :], g_ref[1, k, 1, at, :]], axis=1),
                ], axis=0)
                for rel in range(2):
                    real = outs[rel][k, 0, here, :]
                    imag = outs[rel][k, 1, here, :]
                    wide = jnp.concatenate([
                        jnp.concatenate([real, imag], axis=1),
                        jnp.concatenate([-imag, real], axis=1),
                    ], axis=0)
                    total = None
                    for _ in range(3):
                        piece = wide.astype(jnp.bfloat16)
                        wide = wide - piece.astype(jnp.float32)
                        term = lax.dot_general(factor, piece, (((0,), (0,)), ((), ())),
                                               preferred_element_type=jnp.float32)
                        total = term if total is None else total + term
                    gram_ref[rel, k, 0] += total[:, :BLK]
                    gram_ref[rel, k, 1] += total[:, BLK:]

            return carry

        lax.fori_loop(0, listed, correct, 0)


def products(meta, g, a, listed, blocks_col, blocks_row):
    rows = a.shape[1]
    width = 2 * g.shape[4]
    pairs = (listed + 1) // 2
    half = jax.ShapeDtypeStruct((NSN, 2, rows, BLK), jnp.float32)
    return pl.pallas_call(
        functools.partial(product_kernel, listed, blocks_col, blocks_row),
        out_shape=(half, half, jax.ShapeDtypeStruct((2, NSN, 2, width, BLK), jnp.float32)),
        in_specs=[SMEM, VMEM, ANY],
        out_specs=(VMEM, VMEM, VMEM),
        scratch_shapes=[
            pltpu.VMEM((NSN, pairs, rows, 4 * BLK), jnp.bfloat16),
            pltpu.VMEM((4 * BLK, 4 * BLK), jnp.bfloat16),
            pltpu.SMEM((NSN, listed), jnp.int32),
            pltpu.SemaphoreType.DMA((NSN, pairs)),
        ],
        compiler_params=pltpu.CompilerParams(vmem_limit_bytes=56 * 1024 * 1024),
        name="listed_products",
    )(meta, g, a)


def reduce_kernel(n, oth_ref, gram_ref, recv_ref, sum_ref, pair, mine, parts,
                  p_send, p_recv, g_send, g_recv, r_send, r_recv, b_send, b_recv):
    row = lax.axis_index("row")
    col = lax.axis_index("col")
    sibling = {"col": 1 - col}
    size = sum_ref.shape[0] // n

    barrier = pltpu.get_barrier_semaphore()
    pl.semaphore_signal(barrier, inc=1, device_id=sibling, device_id_type=MESH)
    for d in range(1, n):
        pl.semaphore_signal(barrier, inc=1, device_id={"row": (row + d) % n}, device_id_type=MESH)
    pl.semaphore_wait(barrier, n)

    halves = pltpu.make_async_remote_copy(
        src_ref=gram_ref.at[1], dst_ref=pair, send_sem=g_send, recv_sem=g_recv,
        device_id=sibling, device_id_type=MESH)
    halves.start()
    values = pltpu.make_async_remote_copy(
        src_ref=oth_ref, dst_ref=recv_ref, send_sem=p_send, recv_sem=p_recv,
        device_id=sibling, device_id_type=MESH)
    values.start()
    halves.wait()
    mine[...] = gram_ref[0] + pair[...]

    def at(r):
        return pl.ds(pl.multiple_of(r * size, size), size)

    def scatter(d):
        to = (row + d) % n
        return pltpu.make_async_remote_copy(
            src_ref=mine.at[at(to)], dst_ref=parts.at[d], send_sem=r_send.at[d], recv_sem=r_recv.at[d],
            device_id={"row": to}, device_id_type=MESH)

    def spread(d):
        return pltpu.make_async_remote_copy(
            src_ref=parts.at[0], dst_ref=sum_ref.at[at(row)], send_sem=b_send.at[d], recv_sem=b_recv.at[d],
            device_id={"row": (row + d) % n}, device_id_type=MESH)

    for d in range(1, n):
        scatter(d).start()
    total = mine[at(row), :]
    for d in range(1, n):
        scatter(d).wait_recv()
        total = total + parts[d]
    parts[0] = total
    sum_ref[at(row), :] = total
    for d in range(1, n):
        spread(d).start()
    for d in range(1, n):
        scatter(d).wait_send()
    for d in range(1, n):
        spread(d).wait()
    values.wait()


def reduce(n, oth, gram):
    size = gram.shape[1] * gram.shape[2] * gram.shape[3]
    flat = gram.reshape(2, size, BLK)
    dma = pltpu.SemaphoreType.DMA
    return pl.pallas_call(
        functools.partial(reduce_kernel, n),
        out_shape=(jax.ShapeDtypeStruct(oth.shape, oth.dtype), jax.ShapeDtypeStruct((size, BLK), jnp.float32)),
        in_specs=[ANY, VMEM],
        out_specs=(ANY, VMEM),
        scratch_shapes=[
            pltpu.VMEM((size, BLK), jnp.float32),
            pltpu.VMEM((size, BLK), jnp.float32),
            pltpu.VMEM((n, size // n, BLK), jnp.float32),
            dma, dma, dma, dma, dma((n,)), dma((n,)), dma((n,)), dma((n,)),
        ],
        compiler_params=pltpu.CompilerParams(collective_id=1, has_side_effects=True),
        name="reduce_parts",
    )(oth, flat)


def local(n, inverse_pairs, factor_rows, diag_blocks, row_lists, block_order):
    blocks_row = inverse_pairs.shape[1] // BLK
    blocks_col = inverse_pairs.shape[2] // BLK
    listed = row_lists.shape[1]
    col = lax.axis_index("col")
    hits = row_lists[:, :, None] == block_order[None, None, :]
    storage = jnp.arange(block_order.shape[0], dtype=jnp.int32)
    position = jnp.sum(jnp.where(hits, storage, 0), axis=2).astype(jnp.int32)
    meta = jnp.concatenate([
        position - col * blocks_col,
        position - lax.axis_index("row") * blocks_row,
        jnp.full((1, listed), col, jnp.int32),
    ], axis=0)
    g = gather(n, factor_rows)
    own, oth, gram = products(meta, g, inverse_pairs, listed, blocks_col, blocks_row)
    received, correction = reduce(n, oth, gram)
    schur = diag_blocks.astype(jnp.float32) - correction.reshape(diag_blocks.shape)
    return (own + received, schur)


def solution(mesh):
    in_specs = (
        P("pole", "row", "col"),
        P("pole", None, "row", "col"),
        P("pole", None, None, "col"),
        P(),
        P(),
    )
    out_specs = (P("pole", None, "row", "col"), P("pole", None, None, "col"))
    return jax.shard_map(functools.partial(local, mesh.shape["row"]), mesh=mesh, in_specs=in_specs,
                         out_specs=out_specs, check_vma=False)
```

time: 265 us -> 101 us (0.38); the launches traced: 262 us -> 101 us
  waiting for transfers between devices: 138 us -> 0 us
  Pallas kernels: 0 us -> 94 us
  matrix products: 72 us -> 0 us
  local copies, waits for them, and re-layouts: 24.8 us -> 0.09 us
  between operations: 13.9 us -> 0.7 us
  other arithmetic: 13 us -> 6.32 us
    pallas_call x0 -> x3, Pallas kernels: none -> 94 us  [the longest x1 35.1 us: gather(): pl.pallas_call(functools.partial(gather_kernel, n, ny), out_shape=jax.Sha...]
    dot_general x4 -> x0, matrix products: 72 us -> none  [the longest x1 48 us: local(): jnp.einsum('prc,kqcw->kpqrw', inverse_pairs, column_factor, preferred_ele...]
    psum x1 -> x0, waiting for transfers between devices: 69 us -> none  [local(): correction = lax.psum(complex_gram(row_factor, values), 'row')]
    all_gather x2 -> x0, waiting for transfers between devices: 64.5 us -> none  [the longest x1 50.8 us: local(): lengthened = lax.all_gather(factor_rows, 'row', axis=2, tiled=True)]
    convert_element_type x1 -> x0, local copies, waits for them, and re-layouts: 12.5 us -> none  [local(): column_factor = place_rows(factor_full, row_lists, block_order, col_block...]
    transpose x1 -> x0, local copies, waits for them, and re-layouts: 7.29 us -> none  [place_rows(): jnp.einsum('ktj,kpjbw->kptbw', matches, blocked, preferred_element_type=j...]
    unnamed x9 -> x6, local copies, waits for them, and re-layouts: 4.97 us -> 0.02 us
    another operation x2 -> x0, other arithmetic: 3.92 us -> none  [the longest x1 3.09 us: local(): partial_value = jnp.stack([partial_real, partial_imag], axis=1)]
  transfers between devices with their start and end apart: 4 -> 0, of which waited for: 4 -> 0; matrix products, arithmetic and copies ran while one was open for 6% -> 0% of each run, Pallas kernels for 0% -> 0%
where the time goes in v1:
time: 101 us
  Pallas kernels  94 us (93%)
  other arithmetic  6.32 us (6%)
    pallas_call x1, Pallas kernels, gather(): pl.pallas_call(functools.partial(gather_kernel, n, ny), out_shape=jax.Sha...  35.1 us
    pallas_call x1, Pallas kernels, reduce(): pl.pallas_call(functools.partial(reduce_kernel, n), out_shape=(jax.ShapeD...  33.6 us
    pallas_call x1, Pallas kernels, products(): pl.pallas_call(functools.partial(product_kernel, listed, blocks_col, bloc...  25.3 us
    add x1, other arithmetic, local(): return (own + received, schur)  3.93 us

profile of v1, /device:TPU:26, one launch (start us, length us, event | category | flops | bytes accessed | tf_op | source)
XLA Modules:
  0.0 101.1 jit_solution(13675528166076698779)
XLA Ops:
  0.6 0.1 pad.2.clone
  0.7 0.9 select_reduce_fusion
  1.6 0.7 add_add_fusion.meta
  2.3 35.1 %gather_factor.1.g_ref = bf16[2,2,2,2048,128]{4,3,2,1,0:T(8,128)(2,1)} custom-call(bf16[2,2,256,128]{3,2,1,0:T(8,128)(2,1)} %x_ref.1), custom_call_target="tpu_custom_call" | custom-call | tf_op jit(solution)/shard_map/gather_factor/pallas_call | solution.py:133
  37.3 25.3 %listed_products.1 = (f32[2,2,1536,128]{3,2,1,0:T(8,128)}, f32[2,2,1536,128]{3,2,1,0:T(8,128)}, f32[2,2,2,256,128]{4,3,2,1,0:T(8,128)}) custom-call(s32[5,16]{1,0:T(8,128)} %add_add_fusion.meta, bf16[2,2,2,2048,128]{4,3,2,1,0:T(8,128)(2,1)} %gather_factor.1.g_ref, bf16[2,1536,6144]{2,1,0:T(8,128)(2,1)} %a_ref.1), custom_call_target="tpu_custom_call" | custom-call | tf_op jit(solution)/shard_map/listed_products/pallas_call | solution.py:265
  62.7 0.0 copy-start
  62.7 33.6 %reduce_parts.1 = (f32[2,2,1536,128]{3,2,1,0:T(8,128)}, f32[1024,128]{1,0:T(8,128)}) custom-call(f32[2,2,1536,128]{3,2,1,0:T(8,128)} %get-tuple-element.8.oth_ref, f32[2,1024,128]{2,1,0:T(8,128)} %bitcast.3), custom_call_target="tpu_custom_call" | custom-call | tf_op jit(solution)/shard_map/reduce_parts/pallas_call | solution.py:340
  96.3 0.0 copy-done
  96.3 0.0 copy-start.1
  96.3 0.0 copy-start.2
  96.3 3.9 %add.3 = f32[2,2,1536,128]{3,2,1,0:T(8,128)} add(f32[2,2,1536,128]{3,2,1,0:T(8,128)S(1)} %copy-done, f32[2,2,1536,128]{3,2,1,0:T(8,128)} %get-tuple-element.10) | non-fusion elementwise | flops 786432 | bytes 9437184 | tf_op jit(solution)/shard_map/add | solution.py:373
  100.2 0.0 copy-done.1
  100.2 0.0 copy-done.2
  100.2 0.8 convert_subtract_fusion
  (1 shorter events, 0.0 us)
Async XLA Ops:
  62.7 33.6 %copy-start = (f32[2,2,1536,128]{3,2,1,0:T(8,128)S(1)}, f32[2,2,1536,128]{3,2,1,0:T(8,128)}, u32[]{:S(2)}) copy-start(f32[2,2,1536,128]{3,2,1,0:T(8,128)} %get-tuple-element.7) | copy-start | bytes 9437188
  96.3 4.0 %copy-start.1 = (f32[1024,128]{1,0:T(8,128)S(1)}, f32[1024,128]{1,0:T(8,128)}, u32[]{:S(2)}) copy-start(f32[1024,128]{1,0:T(8,128)} %get-tuple-element.11) | copy-start | bytes 1572868
  96.3 3.9 %copy-start.2 = (bf16[2,2,256,128]{3,2,1,0:T(8,128)(2,1)S(1)}, bf16[2,2,256,128]{3,2,1,0:T(8,128)(2,1)}, u32[]{:S(2)}) copy-start(bf16[2,2,256,128]{3,2,1,0:T(8,128)(2,1)} %param.7) | copy-start | bytes 786436

commit v2 on v0

v2 whole, which is shorter than its diff:
```python
import functools

import jax
import jax.numpy as jnp
from jax import lax
from jax.experimental import pallas as pl
from jax.experimental.pallas import tpu as pltpu
from jax.sharding import PartitionSpec as P

NSN = 2
BLK = 128
MESH = pl.DeviceIdType.MESH
ANY = pl.BlockSpec(memory_space=pl.ANY)
VMEM = pl.BlockSpec(memory_space=pltpu.VMEM)
SMEM = pl.BlockSpec(memory_space=pltpu.SMEM)


def aligned(start, size):
    return pl.ds(pl.multiple_of(start, size), size)


def kernel(n, ny, pick, keep, local_pick, local_keep, x_ref, a_ref, out_ref, sum_ref,
           a_buf, g_ref, own, oth, recv, bbuf, mine, parts,
           a_sem, loc_sem, z_send, z_recv, y_send, y_recv, s_send, s_recv,
           v_send, v_recv, o_sem, r_send, r_recv, b_send, b_recv):
    nz = n // ny
    span = g_ref.shape[3] * BLK // n
    rows = a_ref.shape[1]
    blocks_col = a_ref.shape[2] // BLK
    blocks_row = rows // BLK
    tile = 512 if rows % 512 == 0 else 384 if rows % 384 == 0 else BLK
    per = max(1, span // BLK)
    unit = min(span, BLK)
    row = lax.axis_index("row")
    col = lax.axis_index("col")
    z = row // ny
    y = row % ny
    oy = ny - 1 - y
    sibling = {"col": 1 - col}
    up = {"row": row + ny}
    down = {"row": row - ny}
    across = {"row": z * ny + oy}

    def stream(b):
        return pltpu.make_async_copy(a_ref.at[:, :, aligned(b * BLK, BLK)], a_buf.at[b], a_sem.at[b])

    def start_stream(b, carry):
        stream(b).start()
        return carry

    def wait_stream(b, carry):
        stream(b).wait()
        return carry

    def slot(c, r):
        if span >= BLK:
            return g_ref.at[c, :, :, pl.ds(r * per, per)]
        return g_ref.at[c, :, :, r * span // BLK, aligned(r * span % BLK, span)]

    local = pltpu.make_async_copy(x_ref, slot(col, row), loc_sem)
    local.start()

    barrier = pltpu.get_barrier_semaphore()
    pl.semaphore_signal(barrier, inc=1, device_id=sibling, device_id_type=MESH)
    for d in range(1, n):
        pl.semaphore_signal(barrier, inc=1, device_id={"row": (row + d) % n}, device_id_type=MESH)
    pl.semaphore_wait(barrier, n)

    def copy(src, c, r, send, got, target):
        return pltpu.make_async_remote_copy(
            src_ref=src, dst_ref=slot(c, r), send_sem=send, recv_sem=got,
            device_id=target, device_id_type=MESH)

    def line(src, zz, target):
        return copy(src, col, zz * ny + y, z_send.at[zz], z_recv.at[zz], target)

    def side(src, zz, yy):
        return copy(src, col, zz * ny + yy, y_send.at[zz], y_recv.at[zz], across)

    def sib(src, c, r):
        return copy(src, c, r, s_send.at[r], s_recv.at[r], sibling)

    def here(zz, yy):
        return slot(col, zz * ny + yy)

    first_up = copy(x_ref, col, row, z_send.at[nz], z_recv.at[z], up)
    first_down = copy(x_ref, col, row, z_send.at[nz + 1], z_recv.at[z], down)
    pl.when(z < nz - 1)(lambda: first_up.start())
    pl.when(z > 0)(lambda: first_down.start())
    side(x_ref, z, y).start()
    sib(x_ref, col, row).start()
    lax.fori_loop(0, blocks_col, start_stream, 0)
    own[...] = jnp.zeros_like(own)
    oth[...] = jnp.zeros_like(oth)
    mine[...] = jnp.zeros_like(mine)
    local.wait()

    def from_line(zz, forward, target):
        line(here(zz, y), zz, target).wait_recv()

        @pl.when(forward)
        def _():
            line(here(zz, y), zz, target).start()

        side(here(zz, y), zz, y).start()
        sib(here(zz, y), col, zz * ny + y).start()

    def from_side(zz):
        side(here(zz, oy), zz, oy).wait_recv()
        sib(here(zz, oy), col, zz * ny + oy).start()

    outs = (own, oth)

    def multiply(r):
        sib(slot(1 - col, r), 1 - col, r).wait_recv()

        def supernode(k, carry):
            if unit < BLK:
                bbuf[...] = jnp.zeros_like(bbuf)
            for e in range(per):
                start = r * span + e * BLK
                scale = keep[k, start // BLK]
                base = e * 2 * BLK
                if unit < BLK:
                    shift = start % BLK
                    top = aligned(base + shift, unit)
                    low = aligned(base + BLK + shift, unit)
                else:
                    top = pl.ds(base, unit)
                    low = pl.ds(base + BLK, unit)
                for rel in range(2):
                    c = col if rel == 0 else 1 - col
                    at = pl.ds(0, unit) if unit == BLK else aligned(start % BLK, unit)
                    real = (g_ref[c, k, 0, start // BLK, at, :].astype(jnp.float32) * scale).astype(jnp.bfloat16)
                    imag = (g_ref[c, k, 1, start // BLK, at, :].astype(jnp.float32) * scale).astype(jnp.bfloat16)
                    left = rel * 2 * BLK
                    bbuf[top, left:left + BLK] = -real
                    bbuf[top, left + BLK:left + 2 * BLK] = -imag
                    bbuf[low, left:left + BLK] = imag
                    bbuf[low, left + BLK:left + 2 * BLK] = -real

            def by_tile(t, inner):
                at = aligned(t * tile, tile)
                pieces = []
                for e in range(per):
                    block = pick[k, (r * span + e * BLK) // BLK]
                    pieces += [a_buf[block, 0, at, :], a_buf[block, 1, at, :]]
                left = jnp.concatenate(pieces, axis=1)
                for rel in range(2):
                    found = jnp.dot(left, bbuf[:, rel * 2 * BLK:(rel + 1) * 2 * BLK],
                                    preferred_element_type=jnp.float32)
                    outs[rel][k, 0, at, :] += found[:, :BLK]
                    outs[rel][k, 1, at, :] += found[:, BLK:]
                return inner

            lax.fori_loop(0, rows // tile, by_tile, 0)
            return carry

        lax.fori_loop(0, NSN, supernode, 0)

    def one_round(d, carry):
        pl.when(z - d >= 0)(lambda: from_line(z - d, z < nz - 1, up))
        pl.when(z + d < nz)(lambda: from_line(z + d, z > 0, down))
        pl.when(z - d + 1 >= 0)(lambda: from_side(z - d + 1))
        pl.when((d > 1) & (z + d - 1 < nz))(lambda: from_side(z + d - 1))

        @pl.when(d == 2)
        def _():
            lax.fori_loop(0, blocks_col, wait_stream, 0)


        def late(q, inner):
            away = d - 2 - q // 2
            zz = z + jnp.where(q % 2 == 0, -away, away)
            yy = jnp.where(q // 2 == 0, y, oy)
            valid = (away >= 0) & (zz >= 0) & (zz < nz) & ((away > 0) | (q % 2 == 0))
            pl.when(valid)(lambda: multiply(zz * ny + yy))
            return inner

        lax.fori_loop(0, 4, late, 0)
        return carry

    lax.fori_loop(1, nz + 3, one_round, 0)

    def swap(k):
        return pltpu.make_async_remote_copy(
            src_ref=oth.at[k], dst_ref=recv.at[k], send_sem=v_send.at[k], recv_sem=v_recv.at[k],
            device_id=sibling, device_id_type=MESH)

    for k in range(NSN):
        swap(k).start()
    for r in range(n):
        sib(slot(col, r), col, r).wait_send()
    for zz in range(nz):
        side(here(zz, y), zz, y).wait_send()
        pl.when(((zz < z) & (z < nz - 1)) | ((zz > z) & (z > 0)))(
            lambda: line(here(zz, y), zz, up).wait_send())
    pl.when(z < nz - 1)(lambda: first_up.wait_send())
    pl.when(z > 0)(lambda: first_down.wait_send())

    group = 3 if blocks_row % 3 == 0 else 1
    width = 2 * BLK
    for k in range(NSN):
        swap(k).wait_recv()
        own[k] += recv[k]
        pltpu.make_async_copy(own.at[k], out_ref.at[k], o_sem.at[k]).start()

        def correct(s, carry, k=k):
            left, right = [], []
            for u in range(group):
                t = s * group + u
                j = local_pick[k, t]
                scale = local_keep[k, t]
                for p in range(2):
                    left.append(jnp.concatenate([g_ref[0, k, p, j], g_ref[1, k, p, j]], axis=1))
                real = own[k, 0, aligned(t * BLK, BLK), :] * scale
                imag = own[k, 1, aligned(t * BLK, BLK), :] * scale
                right.append(jnp.concatenate([real, imag], axis=1))
                right.append(jnp.concatenate([-imag, real], axis=1))
            factor = jnp.concatenate(left, axis=0)
            wide = jnp.concatenate(right, axis=0)
            total = None
            for _ in range(3):
                piece = wide.astype(jnp.bfloat16)
                wide = wide - piece.astype(jnp.float32)
                term = lax.dot_general(factor, piece, (((0,), (0,)), ((), ())),
                                       preferred_element_type=jnp.float32)
                total = term if total is None else total + term
            mine[2 * k * width:(2 * k + 1) * width, :] += total[:, :BLK]
            mine[(2 * k + 1) * width:(2 * k + 2) * width, :] += total[:, BLK:]
            return carry

        lax.fori_loop(0, blocks_row // group, correct, 0)

    size = sum_ref.shape[0] // n

    def scatter(d):
        to = (row + d) % n
        return pltpu.make_async_remote_copy(
            src_ref=mine.at[aligned(to * size, size)], dst_ref=parts.at[d],
            send_sem=r_send.at[d], recv_sem=r_recv.at[d],
            device_id={"row": to}, device_id_type=MESH)

    def spread(d):
        return pltpu.make_async_remote_copy(
            src_ref=parts.at[0], dst_ref=sum_ref.at[aligned(row * size, size)],
            send_sem=b_send.at[d], recv_sem=b_recv.at[d],
            device_id={"row": (row + d) % n}, device_id_type=MESH)

    for d in range(1, n):
        scatter(d).start()
    total = mine[aligned(row * size, size), :]
    for d in range(1, n):
        scatter(d).wait_recv()
        total = total + parts[d]
    parts[0] = total
    sum_ref[aligned(row * size, size), :] = total
    for d in range(1, n):
        spread(d).start()
    for k in range(NSN):
        swap(k).wait_send()
        pltpu.make_async_copy(own.at[k], out_ref.at[k], o_sem.at[k]).wait()
    for d in range(1, n):
        scatter(d).wait_send()
    for d in range(1, n):
        spread(d).wait()


def local(n, inverse_pairs, factor_rows, diag_blocks, row_lists, block_order):
    rows, cols = inverse_pairs.shape[1:]
    blocks_row, blocks_col = rows // BLK, cols // BLK
    listed = row_lists.shape[1]
    hits = row_lists[:, :, None] == block_order[None, None, :]
    storage = jnp.arange(block_order.shape[0], dtype=jnp.int32)
    position = jnp.sum(jnp.where(hits, storage, 0), axis=2).astype(jnp.int32)
    pick = position - lax.axis_index("col") * blocks_col
    keep = ((pick >= 0) & (pick < blocks_col)).astype(jnp.float32)
    pick = jnp.clip(pick, 0, blocks_col - 1)
    place = lax.axis_index("row") * blocks_row + jnp.arange(blocks_row, dtype=jnp.int32)
    found = position[:, None, :] == place[None, :, None]
    local_pick = jnp.sum(jnp.where(found, jnp.arange(listed, dtype=jnp.int32), 0), axis=2).astype(jnp.int32)
    local_keep = jnp.sum(found.astype(jnp.float32), axis=2)

    ny = 2 if n % 2 == 0 else 1
    nz = n // ny
    span, half = factor_rows.shape[2:]
    size = NSN * 2 * 2 * half
    per = max(1, span // BLK)
    shards = factor_rows.reshape(NSN, 2, per, BLK, half) if span >= BLK else factor_rows
    dma = pltpu.SemaphoreType.DMA
    side = (NSN, 2, rows, half)
    values, correction = pl.pallas_call(
        functools.partial(kernel, n, ny),
        out_shape=(jax.ShapeDtypeStruct(side, jnp.float32), jax.ShapeDtypeStruct((size, half), jnp.float32)),
        in_specs=[SMEM, SMEM, SMEM, SMEM, ANY, ANY],
        out_specs=(ANY, VMEM),
        scratch_shapes=[
            pltpu.VMEM((blocks_col, 2, rows, BLK), jnp.bfloat16),
            pltpu.VMEM((2, NSN, 2, listed, BLK, half), jnp.bfloat16),
            pltpu.VMEM(side, jnp.float32),
            pltpu.VMEM(side, jnp.float32),
            pltpu.VMEM(side, jnp.float32),
            pltpu.VMEM((per * 2 * BLK, 4 * BLK), jnp.bfloat16),
            pltpu.VMEM((size, half), jnp.float32),
            pltpu.VMEM((n, size // n, half), jnp.float32),
            dma((blocks_col,)), dma, dma((nz + 2,)), dma((nz,)), dma((nz,)), dma((nz,)), dma((n,)), dma((n,)),
            dma((NSN,)), dma((NSN,)), dma((NSN,)), dma((n,)), dma((n,)), dma((n,)), dma((n,)),
        ],
        compiler_params=pltpu.CompilerParams(
            collective_id=0, has_side_effects=True, vmem_limit_bytes=66000000),
        name="inversion_step",
    )(pick, keep, local_pick, local_keep, shards, inverse_pairs)
    schur = diag_blocks.astype(jnp.float32) - correction.reshape(diag_blocks.shape)
    return (values, schur)


def solution(mesh):
    in_specs = (
        P("pole", "row", "col"),
        P("pole", None, "row", "col"),
        P("pole", None, None, "col"),
        P(),
        P(),
    )
    out_specs = (P("pole", None, "row", "col"), P("pole", None, None, "col"))
    return jax.shard_map(functools.partial(local, mesh.shape["row"]), mesh=mesh, in_specs=in_specs,
                         out_specs=out_specs, check_vma=False)
```

time: 265 us -> 95 us (0.36)
  the two profiles are of different devices: /device:TPU:26 before, /device:TPU:16 now
where the time goes in v2:
time: 95 us; the launch traced here: 94.8 us
  Pallas kernels  84.6 us (89%)
  local copies, waits for them, and re-layouts  5.12 us (5%)
  other arithmetic  4.42 us (5%)
    pallas_call x1, Pallas kernels, local(): pl.pallas_call(functools.partial(kernel, n, ny), out_shape=(jax.ShapeDtyp...  84.6 us
    unnamed x3, local copies, waits for them, and re-layouts  3.76 us

profile of v2, /device:TPU:16, one launch (start us, length us, event | category | flops | bytes accessed | tf_op | source)
XLA Modules:
  0.0 94.8 jit_solution(442076912407996853)
XLA Ops:
  0.6 0.9 select_reduce_fusion
  1.5 0.6 and_convert_fusion.keep
  2.1 0.6 subtract_clamp_fusion.pick
  2.7 0.2 fusion.1
  2.8 0.7 copy.8.local_keep
  3.5 0.3 fusion
  3.9 0.7 copy.7.local_pick
  4.5 0.0 copy-start
  4.5 84.6 %inversion_step.1 = (f32[2,2,1536,128]{3,2,1,0:T(8,128)}, f32[1024,128]{1,0:T(8,128)}) custom-call(s32[2,16]{1,0:T(2,128)} %subtract_clamp_fusion.pick, f32[2,16]{1,0:T(2,128)} %and_convert_fusion.keep, s32[2,12]{1,0:T(2,128)} %copy.7.local_pick, f32[2,12]{1,0:T(2,128)} %copy.8.local_keep, bf16[2,2,2,128,128]{4,3,2,1,0:T(8,128)(2,1)} %bitcast.3, ...), custom_call_target="tpu_custom_call" | custom-call | tf_op jit(solution)/shard_map/inversion_step/pallas_call | solution.py:292
  89.1 0.0 copy-done
  89.1 1.9 %convert_subtract_fusion = f32[2,2,256,128]{3,2,1,0:T(8,128)} fusion(f32[2,2,256,128]{3,2,1,0:T(8,128)} %bitcast.2, bf16[2,2,256,128]{3,2,1,0:T(8,128)(2,1)S(1)} %copy-done), kind=kLoop, calls=%fused_computation | loop fusion | flops 262144 | bytes 1310720 | tf_op jit(solution)/shard_map/sub | solution.py:313
  91.0 3.8 %copy.10 = f32[2,2,1536,128]{3,2,1,0:T(8,128)} copy(f32[2,2,1536,128]{3,2,1,0:T(8,128)} %get-tuple-element.8) | data formatting | bytes 6291456
  (1 shorter events, 0.0 us)
Async XLA Ops:
  4.5 84.6 %copy-start = (bf16[2,2,256,128]{3,2,1,0:T(8,128)(2,1)S(1)}, bf16[2,2,256,128]{3,2,1,0:T(8,128)(2,1)}, u32[]{:S(2)}) copy-start(bf16[2,2,256,128]{3,2,1,0:T(8,128)(2,1)} %param.7) | copy-start | bytes 786436

commit v3 on v2

--- a/solution.py
+++ b/solution.py
@@ -198,6 +198,24 @@
     pl.when(z < nz - 1)(lambda: first_up.wait_send())
     pl.when(z > 0)(lambda: first_down.wait_send())
 
+    size = sum_ref.shape[0] // (NSN * n)
+
+    def place(k, r):
+        return aligned(k * n * size + r * size, size)
+
+    def scatter(k, d):
+        to = (row + d) % n
+        return pltpu.make_async_remote_copy(
+            src_ref=mine.at[place(k, to)], dst_ref=parts.at[k, d],
+            send_sem=r_send.at[k, d], recv_sem=r_recv.at[k, d],
+            device_id={"row": to}, device_id_type=MESH)
+
+    def spread(k, d):
+        return pltpu.make_async_remote_copy(
+            src_ref=parts.at[k, 0], dst_ref=sum_ref.at[place(k, row)],
+            send_sem=b_send.at[k, d], recv_sem=b_recv.at[k, d],
+            device_id={"row": (row + d) % n}, device_id_type=MESH)
+
     group = 3 if blocks_row % 3 == 0 else 1
     width = 2 * BLK
     for k in range(NSN):
@@ -220,7 +238,7 @@
             factor = jnp.concatenate(left, axis=0)
             wide = jnp.concatenate(right, axis=0)
             total = None
-            for _ in range(3):
+            for _ in range(2):
                 piece = wide.astype(jnp.bfloat16)
                 wide = wide - piece.astype(jnp.float32)
                 term = lax.dot_general(factor, piece, (((0,), (0,)), ((), ())),
@@ -231,39 +249,25 @@
             return carry
 
         lax.fori_loop(0, blocks_row // group, correct, 0)
-
-    size = sum_ref.shape[0] // n
-
-    def scatter(d):
-        to = (row + d) % n
-        return pltpu.make_async_remote_copy(
-            src_ref=mine.at[aligned(to * size, size)], dst_ref=parts.at[d],
-            send_sem=r_send.at[d], recv_sem=r_recv.at[d],
-            device_id={"row": to}, device_id_type=MESH)
-
-    def spread(d):
-        return pltpu.make_async_remote_copy(
-            src_ref=parts.at[0], dst_ref=sum_ref.at[aligned(row * size, size)],
-            send_sem=b_send.at[d], recv_sem=b_recv.at[d],
-            device_id={"row": (row + d) % n}, device_id_type=MESH)
-
-    for d in range(1, n):
-        scatter(d).start()
-    total = mine[aligned(row * size, size), :]
-    for d in range(1, n):
-        scatter(d).wait_recv()
-        total = total + parts[d]
-    parts[0] = total
-    sum_ref[aligned(row * size, size), :] = total
-    for d in range(1, n):
-        spread(d).start()
+        for d in range(1, n):
+            scatter(k, d).start()
+
+
+    for k in range(NSN):
+        total = mine[place(k, row), :]
+        for d in range(1, n):
+            scatter(k, d).wait_recv()
+            total = total + parts[k, d]
+        parts[k, 0] = total
+        sum_ref[place(k, row), :] = total
+        for d in range(1, n):
+            spread(k, d).start()
     for k in range(NSN):
         swap(k).wait_send()
         pltpu.make_async_copy(own.at[k], out_ref.at[k], o_sem.at[k]).wait()
-    for d in range(1, n):
-        scatter(d).wait_send()
-    for d in range(1, n):
-        spread(d).wait()
+        for d in range(1, n):
+            scatter(k, d).wait_send()
+            spread(k, d).wait()
 
 
 def local(n, inverse_pairs, factor_rows, diag_blocks, row_lists, block_order):
@@ -302,9 +306,9 @@
             pltpu.VMEM(side, jnp.float32),
             pltpu.VMEM((per * 2 * BLK, 4 * BLK), jnp.bfloat16),
             pltpu.VMEM((size, half), jnp.float32),
-            pltpu.VMEM((n, size // n, half), jnp.float32),
+            pltpu.VMEM((NSN, n, size // (NSN * n), half), jnp.float32),
             dma((blocks_col,)), dma, dma((nz + 2,)), dma((nz,)), dma((nz,)), dma((nz,)), dma((n,)), dma((n,)),
-            dma((NSN,)), dma((NSN,)), dma((NSN,)), dma((n,)), dma((n,)), dma((n,)), dma((n,)),
+            dma((NSN,)), dma((NSN,)), dma((NSN,)), dma((NSN, n)), dma((NSN, n)), dma((NSN, n)), dma((NSN, n)),
         ],
         compiler_params=pltpu.CompilerParams(
             collective_id=0, has_side_effects=True, vmem_limit_bytes=66000000),

time: 95 us -> 86.7 us (0.913)
  the two profiles are of different devices: /device:TPU:16 before, /device:TPU:26 now
where the time goes in v3:
time: 86.7 us; the launch traced here: 85.6 us
  Pallas kernels  75.4 us (87%)
  local copies, waits for them, and re-layouts  5.12 us (6%)
  other arithmetic  4.42 us (5%)
    pallas_call x1, Pallas kernels, local(): pl.pallas_call(functools.partial(kernel, n, ny), out_shape=(jax.ShapeDtyp...  75.4 us
    unnamed x3, local copies, waits for them, and re-layouts  3.76 us
    sub x1, other arithmetic, local(): diag_blocks.astype(jnp.float32) - correction.reshape(diag_blocks.shape)  1.9 us

profile of v3, /device:TPU:26, one launch (start us, length us, event | category | flops | bytes accessed | tf_op | source)
XLA Modules:
  0.0 85.6 jit_solution(8461332454575901663)
XLA Ops:
  0.6 0.9 %select_reduce_fusion = s32[2,16]{1,0:T(2,128)S(1)} fusion(s32[96]{0:T(128)} %param.9, s32[2,16]{1,0:T(2,128)} %param.8), kind=kLoop, calls=%fused_computation.3 | loop fusion | flops 9184 | bytes 640 | tf_op jit(solution)/shard_map/reduce_sum | solution.py:279
  1.5 0.6 and_convert_fusion.keep
  2.1 0.6 subtract_clamp_fusion.pick
  2.7 0.2 fusion.1
  2.8 0.7 copy.8.local_keep
  3.5 0.3 fusion
  3.9 0.7 copy.7.local_pick
  4.5 0.0 copy-start
  4.5 75.4 %inversion_step.1 = (f32[2,2,1536,128]{3,2,1,0:T(8,128)}, f32[1024,128]{1,0:T(8,128)}) custom-call(s32[2,16]{1,0:T(2,128)} %subtract_clamp_fusion.pick, f32[2,16]{1,0:T(2,128)} %and_convert_fusion.keep, s32[2,12]{1,0:T(2,128)} %copy.7.local_pick, f32[2,12]{1,0:T(2,128)} %copy.8.local_keep, bf16[2,2,2,128,128]{4,3,2,1,0:T(8,128)(2,1)} %bitcast.3, ...), custom_call_target="tpu_custom_call" | custom-call | tf_op jit(solution)/shard_map/inversion_step/pallas_call | solution.py:296
  79.9 0.0 copy-done
  79.9 1.9 %convert_subtract_fusion = f32[2,2,256,128]{3,2,1,0:T(8,128)} fusion(f32[2,2,256,128]{3,2,1,0:T(8,128)} %bitcast.2, bf16[2,2,256,128]{3,2,1,0:T(8,128)(2,1)S(1)} %copy-done), kind=kLoop, calls=%fused_computation | loop fusion | flops 262144 | bytes 1310720 | tf_op jit(solution)/shard_map/sub | solution.py:317
  81.8 3.8 %copy.10 = f32[2,2,1536,128]{3,2,1,0:T(8,128)} copy(f32[2,2,1536,128]{3,2,1,0:T(8,128)} %get-tuple-element.8) | data formatting | bytes 6291456
  (1 shorter events, 0.0 us)
Async XLA Ops:
  4.5 75.4 %copy-start = (bf16[2,2,256,128]{3,2,1,0:T(8,128)(2,1)S(1)}, bf16[2,2,256,128]{3,2,1,0:T(8,128)(2,1)}, u32[]{:S(2)}) copy-start(bf16[2,2,256,128]{3,2,1,0:T(8,128)(2,1)} %param.7) | copy-start | bytes 786436
